TPU v7x, 512 devices: a whole 4x8x8 slice. The times are simulated.
512 devices in a mesh: dp: 2 (over z_hi), ctx: 32 (over z_lo, y), tp: 8 (over x, core).
Axes of the slice: x: 4, y: 8, z: 8 (z_hi: 2, z_lo: 4; z = z_hi * 4 + z_lo), core: 2. Of those that a mesh axis runs over, the one named last changes fastest.
Arguments:
- left_stream: bfloat16 [2, 4096, 4096], P('dp', 'ctx', 'tp'), may hold values from -6 to 6
- outer_gate: bfloat16 [2, 4096, 4096], P('dp', 'ctx', 'tp'), may hold values from -6 to 6
- value_stream: bfloat16 [2, 4096, 4096], P('dp', 'ctx', 'tp'), may hold values from -6 to 6
- residual: bfloat16 [2, 4096, 4096], P('dp', 'ctx', 'tp'), may hold values from -36 to 36
- long_filter: float32 [256, 128], P('tp'), may hold values from -2 to 2
- skip_weight: float32 [4096], P('tp'), may hold values from -1 to 1
- norm_gain: float32 [4096], P('tp'), may hold values from 0.1 to 1.9
- normed_grad: bfloat16 [2, 4096, 4096], P('dp', 'ctx', 'tp'), may hold values from -6 to 6
- attn_queries: bfloat16 [2, 4096, 4096], P('dp', 'ctx', 'tp'), may hold values from -6 to 6
- attn_keys: bfloat16 [2, 4096, 4096], P('dp', 'ctx', 'tp'), may hold values from -6 to 6
- attn_values: bfloat16 [2, 4096, 4096], P('dp', 'ctx', 'tp'), may hold values from -6 to 6
- attended_grad: bfloat16 [2, 4096, 4096], P('dp', 'ctx', 'tp'), may hold values from -6 to 6
Outputs:
- normed: bfloat16 [2, 4096, 4096], P('dp', 'ctx', 'tp')
- grad_left: bfloat16 [2, 4096, 4096], P('dp', 'ctx', 'tp')
- grad_outer: bfloat16 [2, 4096, 4096], P('dp', 'ctx', 'tp')
- grad_value: bfloat16 [2, 4096, 4096], P('dp', 'ctx', 'tp')
- grad_residual: bfloat16 [2, 4096, 4096], P('dp', 'ctx', 'tp')
- grad_filter: float32 [256, 128], P('tp')
- grad_skip: float32 [4096], P('tp')
- grad_gain: float32 [4096], P('tp')
- attended: bfloat16 [2, 4096, 4096], P('dp', 'ctx', 'tp')
- grad_queries: bfloat16 [2, 4096, 4096], P('dp', 'ctx', 'tp')
- grad_keys: bfloat16 [2, 4096, 4096], P('dp', 'ctx', 'tp')
- grad_values: bfloat16 [2, 4096, 4096], P('dp', 'ctx', 'tp')
All inputs are finite; a program needn't handle non-finite values.
Results may differ from a plain program's by a relative error of at most 0.024.
Values may be sent and summed in bfloat16 or wider, within the bound.
A program may use at most 128 MiB of HBM per device.

v0:
```python
import jax
import jax.numpy as jnp
from jax import lax
from jax.sharding import PartitionSpec as P

HEAD_DIM = 128


def passed_along(value, axis, steps):
    count = lax.axis_size(axis)
    initial, last = (max(0, -steps), min(count, count - steps))
    return lax.ppermute(value, axis, [(source, source + steps) for source in range(initial, last)])


def toeplitz(taps_rows, rows):
    groups, length = taps_rows.shape
    width = rows + length - 1
    padded = jnp.pad(taps_rows, ((0, 0), (0, width + 1 - length)))
    tiled = jnp.tile(padded, (1, rows))[:, : rows * width]
    return tiled.reshape(groups, rows, width)


def diagonals(matrix, length):
    groups, rows, width = matrix.shape
    flat = jnp.pad(matrix.reshape(groups, rows * width), ((0, 0), (0, rows)))
    return flat.reshape(groups, rows, width + 1)[:, :, :length]


def scores_block(query_rows, key_block, scale):
    return (
        jnp.einsum("rhd,khd->hrk", query_rows, key_block, preferred_element_type=jnp.float32)
        * scale
    )


def key_block_at(key_all, value_all, number, block, positions):
    begin = number * block
    keys_here = lax.dynamic_slice_in_dim(key_all, begin, block, 0)
    values_here = lax.dynamic_slice_in_dim(value_all, begin, block, 0)
    key_pos = begin + jnp.arange(block, dtype=jnp.int32)
    allowed = key_pos[None, :] <= positions[:, None]
    return (keys_here, values_here, allowed)


def attend_rows(query_rows, first_pos, key_all, value_all, block, scale):
    count_rows = query_rows.shape[0]
    heads_here = query_rows.shape[1]
    positions = first_pos + jnp.arange(count_rows, dtype=jnp.int32)
    needed = (first_pos + count_rows - 1) // block + 1

    def first_pass(number, carry):
        running, total = carry
        keys_here, values_here, allowed = key_block_at(key_all, value_all, number, block, positions)
        scores = jnp.where(allowed[None], scores_block(query_rows, keys_here, scale), -jnp.inf)
        newest = jnp.maximum(running, jnp.max(scores, axis=2))
        total = total * jnp.exp(running - newest) + jnp.sum(
            jnp.exp(scores - newest[:, :, None]), axis=2
        )
        return (newest, total)

    start_carry = (
        jnp.full((heads_here, count_rows), -jnp.inf, jnp.float32),
        jnp.zeros((heads_here, count_rows), jnp.float32),
    )
    running, total = lax.fori_loop(0, needed, first_pass, start_carry)
    log_norm = running + jnp.log(total)

    def second_pass(number, output):
        keys_here, values_here, allowed = key_block_at(key_all, value_all, number, block, positions)
        scores = jnp.where(allowed[None], scores_block(query_rows, keys_here, scale), -jnp.inf)
        weights = jnp.exp(scores - log_norm[:, :, None]).astype(jnp.bfloat16)
        return output + jnp.einsum(
            "hrk,khd->rhd", weights, values_here, preferred_element_type=jnp.float32
        )

    output = lax.fori_loop(0, needed, second_pass, jnp.zeros(query_rows.shape, jnp.float32))
    return (output, log_norm)


def shards(
    left_stream,
    outer_gate,
    value_stream,
    residual,
    long_filter,
    skip_weight,
    norm_gain,
    normed_grad,
    attn_queries,
    attn_keys,
    attn_values,
    attended_grad,
):
    rows = left_stream.shape[1]
    channels = left_stream.shape[2]
    groups = long_filter.shape[0]
    taps = long_filter.shape[1]
    per_group = channels // groups
    width = channels * lax.axis_size("tp")
    heads_here = attn_queries.shape[2] // HEAD_DIM
    scale = HEAD_DIM ** (-0.5)
    key_all, value_all = (
        lax.all_gather(attn_keys[0], "ctx", axis=0, tiled=True),
        lax.all_gather(attn_values[0], "ctx", axis=0, tiled=True),
    )
    seq_len = key_all.shape[0]
    key_all = key_all.reshape(seq_len, heads_here, HEAD_DIM)
    value_all = value_all.reshape(seq_len, heads_here, HEAD_DIM)
    left_values = left_stream[0].astype(jnp.float32)
    value_values = value_stream[0].astype(jnp.float32)
    gate_values = outer_gate[0].astype(jnp.float32)
    product = (left_values * value_values).astype(jnp.bfloat16)
    earlier = passed_along(product[rows - (taps - 1) :], "ctx", 1)
    extended_narrow = jnp.concatenate([earlier, product], axis=0).reshape(
        rows + taps - 1, groups, per_group
    )
    extended = extended_narrow.astype(jnp.float32)
    forward_band = toeplitz(long_filter[:, ::-1], rows)
    product_wide = product.astype(jnp.float32)
    mixed = jnp.einsum(
        "gts,sgc->tgc",
        forward_band,
        extended,
        precision=lax.Precision.HIGHEST,
        preferred_element_type=jnp.float32,
    ).reshape(rows, channels)
    mixed = mixed + skip_weight[None, :] * product_wide
    stream = residual[0].astype(jnp.float32) + gate_values * mixed
    square_total = lax.psum(jnp.sum(stream * stream, axis=1), "tp")
    inv_rms = lax.rsqrt(square_total / width + 1e-06)
    scaled = stream * inv_rms[:, None]
    normed = (scaled * norm_gain[None, :]).astype(jnp.bfloat16)
    upstream = normed_grad[0].astype(jnp.float32)
    gain_grad = upstream * norm_gain[None, :]
    norm_dot = lax.psum(jnp.sum(gain_grad * scaled, axis=1), "tp")
    stream_grad = inv_rms[:, None] * (gain_grad - scaled * norm_dot[:, None] / width)
    grad_residual = stream_grad.astype(jnp.bfloat16)
    grad_outer = (stream_grad * mixed).astype(jnp.bfloat16)
    gated = (stream_grad * gate_values).astype(jnp.bfloat16)
    later = passed_along(gated[: taps - 1], "ctx", -1)
    ahead = (
        jnp.concatenate([gated, later], axis=0)
        .astype(jnp.float32)
        .reshape(rows + taps - 1, groups, per_group)
    )
    backward_band = toeplitz(long_filter, rows)
    gated_wide = gated.astype(jnp.float32)
    product_grad = jnp.einsum(
        "gts,sgc->tgc",
        backward_band,
        ahead,
        precision=lax.Precision.HIGHEST,
        preferred_element_type=jnp.float32,
    ).reshape(rows, channels)
    product_grad = product_grad + skip_weight[None, :] * gated_wide
    grad_left = (product_grad * value_values).astype(jnp.bfloat16)
    grad_value = (product_grad * left_values).astype(jnp.bfloat16)
    correlation = jnp.einsum(
        "tgc,sgc->gts",
        gated.reshape(rows, groups, per_group),
        extended_narrow,
        preferred_element_type=jnp.float32,
    )
    filter_part = jnp.sum(diagonals(correlation, taps), axis=1)[:, ::-1]
    skip_part = jnp.sum(gated_wide * product_wide, axis=0)
    gain_part = jnp.sum(upstream * scaled, axis=0)
    filter_sum, skip_sum, gain_sum = lax.psum((filter_part, skip_part, gain_part), ("dp", "ctx"))
    devices = lax.axis_size("ctx")
    index = lax.axis_index("ctx")
    per_block = min(devices, max(1, 512 // rows))
    block = rows * per_block
    own_first = index * rows
    query_rows = attn_queries[0].reshape(rows, heads_here, HEAD_DIM)
    attended_wide, log_norm = attend_rows(query_rows, own_first, key_all, value_all, block, scale)
    attended = attended_wide.astype(jnp.bfloat16)
    out_grad = attended_grad[0].reshape(rows, heads_here, HEAD_DIM)
    delta = jnp.sum(out_grad.astype(jnp.float32) * attended.astype(jnp.float32), axis=2).T
    positions = own_first + jnp.arange(rows, dtype=jnp.int32)
    needed = (own_first + rows - 1) // block + 1

    def query_grad_step(number, running_sum):
        keys_here, values_here, allowed = key_block_at(key_all, value_all, number, block, positions)
        scores = jnp.where(allowed[None], scores_block(query_rows, keys_here, scale), -jnp.inf)
        weights = jnp.exp(scores - log_norm[:, :, None]).astype(jnp.bfloat16)
        value_dots = jnp.einsum(
            "rhd,khd->hrk", out_grad, values_here, preferred_element_type=jnp.float32
        )
        score_grad = (weights.astype(jnp.float32) * (value_dots - delta[:, :, None])).astype(
            jnp.bfloat16
        )
        return running_sum + jnp.einsum(
            "hrk,khd->rhd", score_grad, keys_here, preferred_element_type=jnp.float32
        )

    query_grad = lax.fori_loop(
        0, needed, query_grad_step, jnp.zeros((rows, heads_here, HEAD_DIM), jnp.float32)
    )
    grad_queries = (query_grad * scale).astype(jnp.bfloat16)
    stat_norm, stat_delta = (
        lax.all_gather(log_norm.T, "ctx", axis=0, tiled=True),
        lax.all_gather(delta.T, "ctx", axis=0, tiled=True),
    )
    key_own = attn_keys[0].reshape(rows, heads_here, HEAD_DIM)
    value_own = attn_values[0].reshape(rows, heads_here, HEAD_DIM)
    empty = jnp.zeros((rows, heads_here, HEAD_DIM), jnp.float32)
    piece_query = lax.all_gather(attn_queries[0], "ctx", axis=0, tiled=True)
    piece_grad = lax.all_gather(attended_grad[0], "ctx", axis=0, tiled=True)
    count = piece_query.shape[0]
    stride_rows = 512

    def process(number, totals):
        offset = number * stride_rows
        query_part = lax.dynamic_slice_in_dim(piece_query, offset, stride_rows, 0).reshape(
            stride_rows, heads_here, HEAD_DIM
        )
        grad_part = lax.dynamic_slice_in_dim(piece_grad, offset, stride_rows, 0).reshape(
            stride_rows, heads_here, HEAD_DIM
        )
        norm_part = lax.dynamic_slice_in_dim(stat_norm, offset, stride_rows, 0).T
        delta_part = lax.dynamic_slice_in_dim(stat_delta, offset, stride_rows, 0).T
        query_pos = offset + jnp.arange(stride_rows, dtype=jnp.int32)

        def compute(current):
            key_sum, value_sum = current
            allowed = positions[None, :] <= query_pos[:, None]
            scores = jnp.where(allowed[None], scores_block(query_part, key_own, scale), -jnp.inf)
            weights = jnp.exp(scores - norm_part[:, :, None]).astype(jnp.bfloat16)
            value_dots = jnp.einsum(
                "rhd,khd->hrk", grad_part, value_own, preferred_element_type=jnp.float32
            )
            score_grad = (
                weights.astype(jnp.float32) * (value_dots - delta_part[:, :, None])
            ).astype(jnp.bfloat16)
            value_sum = value_sum + jnp.einsum(
                "hrk,rhd->khd", weights, grad_part, preferred_element_type=jnp.float32
            )
            key_sum = key_sum + jnp.einsum(
                "hrk,rhd->khd", score_grad, query_part, preferred_element_type=jnp.float32
            )
            return (key_sum, value_sum)

        def unchanged(current):
            return current

        reaches = offset + stride_rows - 1 >= own_first
        return lax.cond(reaches, compute, unchanged, totals)

    key_sum, value_sum = lax.fori_loop(0, count // stride_rows, process, (empty, empty))
    grad_keys = (key_sum * scale).astype(jnp.bfloat16)
    grad_values = value_sum.astype(jnp.bfloat16)
    flat = (rows, heads_here * HEAD_DIM)
    return (
        normed[None],
        grad_left[None],
        grad_outer[None],
        grad_value[None],
        grad_residual[None],
        filter_sum,
        skip_sum,
        gain_sum,
        attended.reshape(flat)[None],
        grad_queries.reshape(flat)[None],
        grad_keys.reshape(flat)[None],
        grad_values.reshape(flat)[None],
    )


def solution(mesh):
    in_specs = (
        P("dp", "ctx", "tp"),
        P("dp", "ctx", "tp"),
        P("dp", "ctx", "tp"),
        P("dp", "ctx", "tp"),
        P("tp", None),
        P("tp"),
        P("tp"),
        P("dp", "ctx", "tp"),
        P("dp", "ctx", "tp"),
        P("dp", "ctx", "tp"),
        P("dp", "ctx", "tp"),
        P("dp", "ctx", "tp"),
    )
    out_specs = (
        P("dp", "ctx", "tp"),
        P("dp", "ctx", "tp"),
        P("dp", "ctx", "tp"),
        P("dp", "ctx", "tp"),
        P("dp", "ctx", "tp"),
        P("tp", None),
        P("tp"),
        P("tp"),
        P("dp", "ctx", "tp"),
        P("dp", "ctx", "tp"),
        P("dp", "ctx", "tp"),
        P("dp", "ctx", "tp"),
    )
    return jax.shard_map(shards, mesh=mesh, in_specs=in_specs, out_specs=out_specs, check_vma=False)
```

profile of v0, /device:TPU:8, one launch (start us, length us, event | category | flops | bytes accessed | tf_op | source)
XLA Modules:
  0.0 652.6 jit_solution(11089281187697373970)
XLA Ops:
  7.2 1.7 copy.130
  9.0 1.7 copy.129
  10.7 1.7 copy.131
  13.5 3.5 collective-permute-start
  17.0 1.7 copy.137
  19.9 2.4 copy.177
  22.4 2.2 slice.25
  24.6 9.6 %reshape.385 = f32[32,128,255]{2,1,0:T(8,128)} reshape(f32[32,32640]{1,0:T(8,128)} %slice.25) | data formatting | bytes 8355840 | tf_op jit(solution)/shard_map/reshape | solution.py:20
  35.1 2.4 copy.178
  37.5 2.2 slice.27
  39.8 9.5 %reshape.389 = f32[32,128,255]{2,1,0:T(8,128)} reshape(f32[32,32640]{1,0:T(8,128)} %slice.27) | data formatting | bytes 8355840 | tf_op jit(solution)/shard_map/reshape | solution.py:20
  50.0 4.2 fusion.93
  54.5 14.4 %psum.35 = f32[128]{0:T(128)S(1)} all-reduce(f32[128]{0:T(128)S(1)} %get-tuple-element.951), channel_id=1, replica_groups=mesh['dp'=2,'ctx'=32,'tp'=8] {'tp'}, use_global_device_ids=true, to_apply=%region_1.2 | all-reduce | flops 128 | bytes 1024 | tf_op jit(solution)/shard_map/psum | solution.py:129
  69.1 12.6 %psum.36 = f32[128]{0:T(128)S(1)} all-reduce(f32[128]{0:T(128)S(1)} %get-tuple-element.871), channel_id=1, replica_groups=mesh['dp'=2,'ctx'=32,'tp'=8] {'tp'}, use_global_device_ids=true, to_apply=%region_3.4 | all-reduce | flops 128 | bytes 1024 | tf_op jit(solution)/shard_map/psum | solution.py:135
  81.9 3.1 fusion.81
  85.0 5.2 reshape.391
  90.3 2.5 pad.13
  92.7 3.3 copy.179
  96.0 4.8 collective-permute-start.1
  101.8 1.8 slice_reduce_fusion
  103.7 278.5 %all-reduce.3 = (f32[32,128]{1,0:T(8,128)}, f32[512]{0:T(512)}, f32[512]{0:T(512)}) all-reduce(f32[32,128]{1,0:T(8,128)S(1)} %rev.7, f32[512]{0:T(512)S(1)} %get-tuple-element.947, f32[512]{0:T(512)S(1)} %get-tuple-element.870), channel_id=1, replica_groups=mesh['dp'=2,'ctx'=32,'tp'=8] {'dp','ctx'}, use_global_device_ids=true, to_apply=%region_5.6 | all-reduce | flops 5120 | bytes 40960 | tf_op jit(solution)/shard_map/psum | solution.py:167
  382.3 4.2 fusion.94
  387.5 6.4 copy.135
  393.9 1.7 while.56
  394.1 1.4 fusion.125
  395.7 2.0 while.57
  395.9 1.8 fusion.129
  398.0 3.4 while.58
  398.2 1.4 fusion.135
  399.6 1.8 fusion.136
  402.4 140.3 %all_gather.21 = f32[4096,4]{1,0:T(8,128)S(1)} all-gather(f32[128,4]{1,0:T(8,128)S(1)} %copy.167), channel_id=1, replica_groups=mesh['dp'=2,'ctx'=32,'tp'=8] {'ctx'}, dimensions={0}, use_global_device_ids=true | all-gather | bytes 67584 | tf_op jit(solution)/shard_map/all_gather | solution.py:201
  543.4 74.2 %all_gather.20 = f32[4096,4]{0,1:T(4,128)S(1)} all-gather(f32[128,4]{0,1:T(4,128)S(1)} %bitcast.213), channel_id=1, replica_groups=mesh['dp'=2,'ctx'=32,'tp'=8] {'ctx'}, dimensions={0}, use_global_device_ids=true | all-gather | bytes 67584 | tf_op jit(solution)/shard_map/all_gather | solution.py:200
  617.7 25.9 %while.59 = (s32[]{:T(128)}, f32[128,4,128]{2,0,1:T(8,128)S(1)}, f32[128,4,128]{2,0,1:T(8,128)S(1)}, s32[]{:T(128)}, f32[4096,4]{0,1:T(4,128)S(1)}, /*index=5*/f...) while((s32[]{:T(128)}, f32[128,4,128]{2,0,1:T(8,128)S(1)}, ...), condition=%wide.region_22.23_spmd.clone.clone, body=%wide.region_19.22_spmd.clone.clone.sunk | while | flops 270729856 | bytes 7268725 | solution.py:248
  617.7 3.2 conditional.4
  617.8 1.3 constant_dynamic-slice_fusion
  621.0 3.2 conditional.4
  621.0 1.3 constant_dynamic-slice_fusion
  624.2 3.2 conditional.4
  624.2 1.3 constant_dynamic-slice_fusion
  627.5 3.2 conditional.4
  627.5 1.3 constant_dynamic-slice_fusion
  630.7 3.2 conditional.4
  630.7 1.3 constant_dynamic-slice_fusion
  633.9 3.2 conditional.4
  633.9 1.3 constant_dynamic-slice_fusion
  637.2 3.2 conditional.4
  637.2 1.3 constant_dynamic-slice_fusion
  640.4 3.2 conditional.4
  (177 shorter events, 27.8 us)
Async XLA Ops:
  7.2 380.3 %all-gather.11.cloned.1.call-start = ((), (), s32[]{:S(2)}) async-start(), calls=%async_computation.1 | async-start | bytes 4325376 | tf_op jit(solution)/shard_map/all_gather | solution.py:103
  8.9 386.8 %all-gather.9.cloned.1.call-start = ((), (), s32[]{:S(2)}) async-start(), calls=%async_computation | async-start | bytes 4325376 | tf_op jit(solution)/shard_map/all_gather | solution.py:104
  10.7 607.0 %all-gather.13.cloned.1.call-start = ((), (), s32[]{:S(2)}) async-start(), calls=%async_computation.2 | async-start | bytes 4325376 | tf_op jit(solution)/shard_map/all_gather | solution.py:206
  12.4 605.2 %all-gather.15.cloned.1.call-start = ((), (), s32[]{:S(2)}) async-start(), calls=%async_computation.3 | async-start | bytes 4325376 | tf_op jit(solution)/shard_map/all_gather | solution.py:207
  13.5 36.3 %collective-permute-start = (bf16[127,512]{1,0:T(8,128)(2,1)S(1)}, bf16[127,512]{1,0:T(8,128)(2,1)S(1)}, u32[]{:S(2)}, u32[]{:S(2)}) collective-permute-start(bf16[127,512]{1,0:T(8,128)(2,1)S(1)} %slice_bitcast_fusion), channel_id=1, source_target_pairs={{0,8},{8,16},{16,24},{24,32},{32,40},{40,48},{48,56},{56,64},{64,7... | collective-permute-start | bytes 390152 | tf_op jit(solution)/shard_map/ppermute | solution.py:12
  24.5 9.7 %copy-start.1 = (bf16[1,128,512]{2,1,0:T(8,128)(2,1)S(1)}, bf16[1,128,512]{2,1,0:T(8,128)(2,1)}, u32[]{:S(2)}) copy-start(bf16[1,128,512]{2,1,0:T(8,128)(2,1)} %param.29) | copy-start | bytes 393220
  24.5 9.8 %copy-start.3 = (bf16[1,128,512]{2,1,0:T(8,128)(2,1)S(1)}, bf16[1,128,512]{2,1,0:T(8,128)(2,1)}, u32[]{:S(2)}) copy-start(bf16[1,128,512]{2,1,0:T(8,128)(2,1)} %param.25) | copy-start | bytes 393220
  24.5 9.9 %copy-start = (bf16[1,128,512]{2,1,0:T(8,128)(2,1)S(1)}, bf16[1,128,512]{2,1,0:T(8,128)(2,1)}, u32[]{:S(2)}) copy-start(bf16[1,128,512]{2,1,0:T(8,128)(2,1)} %param.23) | copy-start | bytes 393220
  24.6 10.0 %copy-start.10 = (f32[512]{0:T(512)S(1)}, f32[512]{0:T(512)}, u32[]{:S(2)}) copy-start(f32[512]{0:T(512)} %param.28) | copy-start | bytes 6148
  24.6 10.1 %copy-start.11 = (f32[512]{0:T(512)S(1)}, f32[512]{0:T(512)}, u32[]{:S(2)}) copy-start(f32[512]{0:T(512)} %param.27) | copy-start | bytes 6148
  24.6 10.2 %copy-start.9 = (f32[32,128]{1,0:T(8,128)S(1)}, f32[32,128]{1,0:T(8,128)}, u32[]{:S(2)}) copy-start(f32[32,128]{1,0:T(8,128)} %param.26) | copy-start | bytes 49156
  39.7 9.5 %copy-start.4 = (bf16[1,128,512]{1,2,0:T(8,128)(2,1)S(1)}, bf16[1,128,512]{1,2,0:T(8,128)(2,1)}, u32[]{:S(2)}) copy-start(bf16[1,128,512]{1,2,0:T(8,128)(2,1)} %copy.131) | copy-start | bytes 393220
  39.7 9.6 %copy-start.2 = (bf16[1,128,512]{1,2,0:T(8,128)(2,1)S(1)}, bf16[1,128,512]{1,2,0:T(8,128)(2,1)}, u32[]{:S(2)}) copy-start(bf16[1,128,512]{1,2,0:T(8,128)(2,1)} %copy.137) | copy-start | bytes 393220
  39.7 9.7 %copy-start.6 = (bf16[1,128,512]{1,2,0:T(8,128)(2,1)S(1)}, bf16[1,128,512]{1,2,0:T(8,128)(2,1)}, u32[]{:S(2)}) copy-start(bf16[1,128,512]{1,2,0:T(8,128)(2,1)} %copy.130) | copy-start | bytes 393220
  39.7 9.9 %copy-start.5 = (bf16[1,128,512]{1,2,0:T(8,128)(2,1)S(1)}, bf16[1,128,512]{1,2,0:T(8,128)(2,1)}, u32[]{:S(2)}) copy-start(bf16[1,128,512]{1,2,0:T(8,128)(2,1)} %copy.129) | copy-start | bytes 393220
  96.0 286.1 %collective-permute-start.1 = (bf16[127,512]{1,0:T(8,128)(2,1)S(1)}, bf16[127,512]{1,0:T(8,128)(2,1)S(1)}, u32[]{:S(2)}, u32[]{:S(2)}) collective-permute-start(bf16[127,512]{1,0:T(8,128)(2,1)S(1)} %bitcast.212), channel_id=1, source_target_pairs={{8,0},{16,8},{24,16},{32,24},{40,32},{48,40},{56,48},{64,56},{72,6... | collective-permute-start | bytes 390152 | tf_op jit(solution)/shard_map/ppermute | solution.py:12
  101.8 284.8 %copy-start.7 = (bf16[1,128,512]{2,1,0:T(8,128)(2,1)S(1)}, bf16[1,128,512]{2,1,0:T(8,128)(2,1)}, u32[]{:S(2)}) copy-start(bf16[1,128,512]{2,1,0:T(8,128)(2,1)} %param.24) | copy-start | bytes 393220
  101.8 284.8 %copy-start.8 = (bf16[1,128,512]{2,1,0:T(8,128)(2,1)S(1)}, bf16[1,128,512]{2,1,0:T(8,128)(2,1)}, u32[]{:S(2)}) copy-start(bf16[1,128,512]{2,1,0:T(8,128)(2,1)} %param.22) | copy-start | bytes 393220
Sparse Core Ops, SparseCore 0:
  10.6 144.1 all-gather.10
  157.4 139.1 all-gather.8
  299.2 141.8 all-gather.12
  443.5 144.5 all-gather.14
where the time goes:
time: 654 us; the launch traced here: 653 us
  blocking collectives  520 us (80%)
  local copies, waits for them, and re-layouts  70.3 us (11%)
  matrix products  31.3 us (5%)
  between operations  14.2 us (2%)
  starting transfers between devices  8.48 us (1%)
  other arithmetic  6.97 us (1%)
    psum x1, blocking collectives, shards(): lax.psum((filter_part, skip_part, gain_part), ('dp', 'ctx'))  278 us
    all_gather x1, blocking collectives, shards(): lax.all_gather(delta.T, 'ctx', axis=0, tiled=True)  140 us
    all_gather x1, blocking collectives, shards(): lax.all_gather(log_norm.T, 'ctx', axis=0, tiled=True)  74.2 us
    unnamed x40, local copies, waits for them, and re-layouts  23.3 us
    reshape x2, local copies, waits for them, and re-layouts, toeplitz(): return tiled.reshape(groups, rows, width)  19.1 us
    psum x1, blocking collectives, shards(): square_total = lax.psum(jnp.sum(stream * stream, axis=1), 'tp')  14.4 us
  transfers between devices with their start and end apart: 6, of which 0 were waited for; matrix products, arithmetic and copies ran while one was open for 12% of the time, Pallas kernels for 0%

commit v1 on v0

--- a/solution.py
+++ b/solution.py
@@ -197,7 +197,9 @@
     )
     grad_queries = (query_grad * scale).astype(jnp.bfloat16)
     stat_norm, stat_delta = (
-        lax.all_gather(log_norm.T, "ctx", axis=0, tiled=True),
+        jnp.concatenate(
+            lax.all_to_all(jnp.stack([log_norm.T] * lax.axis_size("ctx")), "ctx", 0, 0), axis=0
+        ),
         lax.all_gather(delta.T, "ctx", axis=0, tiled=True),
     )
     key_own = attn_keys[0].reshape(rows, heads_here, HEAD_DIM)

time: 654 us -> 627 us (0.959)
  the two profiles are of different devices: /device:TPU:8 before, /device:TPU:6 now
where the time goes in v1:
time: 627 us; the launch traced here: 625 us
  blocking collectives  405 us (65%)
  local copies, waits for them, and re-layouts  70.9 us (11%)
  starting transfers between devices  54.2 us (9%)
  waiting for transfers between devices  40.8 us (7%)
  matrix products  31.4 us (5%)
  between operations  14.2 us (2%)
  other arithmetic  6.98 us (1%)
    psum x1, blocking collectives, shards(): lax.psum((filter_part, skip_part, gain_part), ('dp', 'ctx'))  285 us
    all_gather x1, blocking collectives, shards(): lax.all_gather(delta.T, 'ctx', axis=0, tiled=True)  94.8 us
    all_to_all x1, starting transfers between devices, shards(): lax.all_to_all(jnp.stack([log_norm.T] * lax.axis_size('ctx')), 'ctx', 0, 0)  49.3 us
    all_gather x1, waiting for transfers between devices, shards(): piece_grad = lax.all_gather(attended_grad[0], 'ctx', axis=0, tiled=True)  40.7 us
    unnamed x40, local copies, waits for them, and re-layouts  23.3 us
    reshape x2, local copies, waits for them, and re-layouts, toeplitz(): return tiled.reshape(groups, rows, width)  19.1 us
    psum x1, blocking collectives, shards(): norm_dot = lax.psum(jnp.sum(gain_grad * scaled, axis=1), 'tp')  13.2 us
  transfers between devices with their start and end apart: 7, of which 1 were waited for; matrix products, arithmetic and copies ran while one was open for 13% of the time, Pallas kernels for 0%

profile of v1, /device:TPU:6, one launch (start us, length us, event | category | flops | bytes accessed | tf_op | source)
XLA Modules:
  0.0 624.9 jit_solution(15356956441379156511)
XLA Ops:
  7.2 1.7 copy.130
  9.0 1.7 copy.129
  10.7 1.7 copy.131
  13.5 3.5 collective-permute-start
  17.0 1.7 copy.137
  19.9 2.4 copy.177
  22.4 2.2 slice.25
  24.6 9.6 %reshape.390 = f32[32,128,255]{2,1,0:T(8,128)} reshape(f32[32,32640]{1,0:T(8,128)} %slice.25) | data formatting | bytes 8355840 | tf_op jit(solution)/shard_map/reshape | solution.py:20
  35.1 2.4 copy.178
  37.5 2.2 slice.27
  39.8 9.5 %reshape.394 = f32[32,128,255]{2,1,0:T(8,128)} reshape(f32[32,32640]{1,0:T(8,128)} %slice.27) | data formatting | bytes 8355840 | tf_op jit(solution)/shard_map/reshape | solution.py:20
  50.0 4.3 fusion.93
  54.6 12.1 %psum.35 = f32[128]{0:T(128)S(1)} all-reduce(f32[128]{0:T(128)S(1)} %get-tuple-element.951), channel_id=1, replica_groups=mesh['dp'=2,'ctx'=32,'tp'=8] {'tp'}, use_global_device_ids=true, to_apply=%region_1.2 | all-reduce | flops 128 | bytes 1024 | tf_op jit(solution)/shard_map/psum | solution.py:129
  66.9 13.2 %psum.36 = f32[128]{0:T(128)S(1)} all-reduce(f32[128]{0:T(128)S(1)} %get-tuple-element.871), channel_id=1, replica_groups=mesh['dp'=2,'ctx'=32,'tp'=8] {'tp'}, use_global_device_ids=true, to_apply=%region_3.4 | all-reduce | flops 128 | bytes 1024 | tf_op jit(solution)/shard_map/psum | solution.py:135
  80.3 3.1 fusion.81
  83.4 5.2 reshape.396
  88.6 2.5 pad.13
  91.1 3.2 copy.179
  94.3 1.3 collective-permute-start.1
  96.6 1.8 slice_reduce_fusion
  98.5 285.1 %all-reduce.3 = (f32[32,128]{1,0:T(8,128)}, f32[512]{0:T(512)}, f32[512]{0:T(512)}) all-reduce(f32[32,128]{1,0:T(8,128)S(1)} %rev.7, f32[512]{0:T(512)S(1)} %get-tuple-element.947, f32[512]{0:T(512)S(1)} %get-tuple-element.870), channel_id=1, replica_groups=mesh['dp'=2,'ctx'=32,'tp'=8] {'dp','ctx'}, use_global_device_ids=true, to_apply=%region_5.6 | all-reduce | flops 5120 | bytes 40960 | tf_op jit(solution)/shard_map/psum | solution.py:167
  383.7 4.2 fusion.94
  389.0 6.4 %copy.135 = bf16[4096,4,128]{2,0,1:T(8,128)(2,1)} copy(bf16[4096,4,128]{0,2,1:T(8,128)(2,1)} %bitcast.194) | data formatting | bytes 8388608
  395.3 1.7 while.56
  395.5 1.4 fusion.125
  397.1 2.0 while.57
  397.3 1.8 fusion.129
  399.5 3.4 while.58
  399.6 1.4 fusion.135
  401.1 1.8 fusion.136
  403.6 49.3 %all-to-all-start = ((f32[32,128,4]{1,2,0:T(4,128)}), f32[32,128,4]{1,2,0:T(4,128)S(1)}, u32[]{:S(2)}, u32[]{:S(2)}) async-start(f32[32,128,4]{1,2,0:T(4,128)} %stack.2), calls=%async_computation | async-start | bytes 131072 | tf_op jit(solution)/shard_map/all_to_all | solution.py:201
  453.8 94.8 %all_gather.17 = f32[4096,4]{1,0:T(8,128)S(1)} all-gather(f32[128,4]{1,0:T(8,128)S(1)} %copy.167), channel_id=1, replica_groups=mesh['dp'=2,'ctx'=32,'tp'=8] {'ctx'}, dimensions={0}, use_global_device_ids=true | all-gather | bytes 67584 | tf_op jit(solution)/shard_map/all_gather | solution.py:203
  550.0 40.7 %all-gather.15.cloned.1.call-done = bf16[1,4096,512]{1,2,0:T(8,128)(2,1)} async-done(((bf16[1,128,512]{1,2,0:T(8,128)(2,1)}), bf16[1,4096,512]{1,2,0:T(8,128)(2,1)}) %all-gather.15.cloned.1.call-update) | async-done | bytes 4194320 | tf_op jit(solution)/shard_map/all_gather | solution.py:209
  590.7 25.9 %while.59 = (s32[]{:T(128)}, f32[128,4,128]{2,0,1:T(8,128)S(1)}, f32[128,4,128]{2,0,1:T(8,128)S(1)}, s32[]{:T(128)}, f32[4096,4]{0,1:T(4,128)S(1)}, /*index=5*/f...) while((s32[]{:T(128)}, f32[128,4,128]{2,0,1:T(8,128)S(1)}, ...), condition=%wide.region_22.23_spmd.clone.clone, body=%wide.region_19.22_spmd.clone.clone.sunk | while | flops 270729856 | bytes 7268725 | solution.py:250
  590.8 3.2 conditional.4
  590.8 1.3 constant_dynamic-slice_fusion
  594.0 3.2 conditional.4
  594.0 1.3 constant_dynamic-slice_fusion
  597.3 3.2 conditional.4
  597.3 1.3 constant_dynamic-slice_fusion
  600.5 3.2 conditional.4
  600.5 1.3 constant_dynamic-slice_fusion
  603.8 3.2 conditional.4
  603.8 1.3 constant_dynamic-slice_fusion
  607.0 3.2 conditional.4
  607.0 1.3 constant_dynamic-slice_fusion
  610.2 3.2 conditional.4
  613.5 3.2 conditional.4
  (179 shorter events, 29.8 us)
Async XLA Ops:
  7.2 381.8 %all-gather.11.cloned.1.call-start = ((), (), s32[]{:S(2)}) async-start(), calls=%async_computation.2 | async-start | bytes 4325376 | tf_op jit(solution)/shard_map/all_gather | solution.py:103
  8.9 388.2 %all-gather.9.cloned.1.call-start = ((), (), s32[]{:S(2)}) async-start(), calls=%async_computation.1 | async-start | bytes 4325376 | tf_op jit(solution)/shard_map/all_gather | solution.py:104
  10.7 539.3 %all-gather.13.cloned.1.call-start = ((), (), s32[]{:S(2)}) async-start(), calls=%async_computation.3 | async-start | bytes 4325376 | tf_op jit(solution)/shard_map/all_gather | solution.py:208
  12.4 578.3 %all-gather.15.cloned.1.call-start = ((), (), s32[]{:S(2)}) async-start(), calls=%async_computation.4 | async-start | bytes 4325376 | tf_op jit(solution)/shard_map/all_gather | solution.py:209
  13.5 36.3 %collective-permute-start = (bf16[127,512]{1,0:T(8,128)(2,1)S(1)}, bf16[127,512]{1,0:T(8,128)(2,1)S(1)}, u32[]{:S(2)}, u32[]{:S(2)}) collective-permute-start(bf16[127,512]{1,0:T(8,128)(2,1)S(1)} %slice_bitcast_fusion), channel_id=1, source_target_pairs={{0,8},{8,16},{16,24},{24,32},{32,40},{40,48},{48,56},{56,64},{64,7... | collective-permute-start | bytes 390152 | tf_op jit(solution)/shard_map/ppermute | solution.py:12
  24.6 9.7 %copy-start.1 = (bf16[1,128,512]{2,1,0:T(8,128)(2,1)S(1)}, bf16[1,128,512]{2,1,0:T(8,128)(2,1)}, u32[]{:S(2)}) copy-start(bf16[1,128,512]{2,1,0:T(8,128)(2,1)} %param.29) | copy-start | bytes 393220
  24.6 9.8 %copy-start.3 = (bf16[1,128,512]{2,1,0:T(8,128)(2,1)S(1)}, bf16[1,128,512]{2,1,0:T(8,128)(2,1)}, u32[]{:S(2)}) copy-start(bf16[1,128,512]{2,1,0:T(8,128)(2,1)} %param.25) | copy-start | bytes 393220
  24.6 9.9 %copy-start = (bf16[1,128,512]{2,1,0:T(8,128)(2,1)S(1)}, bf16[1,128,512]{2,1,0:T(8,128)(2,1)}, u32[]{:S(2)}) copy-start(bf16[1,128,512]{2,1,0:T(8,128)(2,1)} %param.23) | copy-start | bytes 393220
  24.6 10.0 %copy-start.10 = (f32[512]{0:T(512)S(1)}, f32[512]{0:T(512)}, u32[]{:S(2)}) copy-start(f32[512]{0:T(512)} %param.28) | copy-start | bytes 6148
  24.6 10.1 %copy-start.11 = (f32[512]{0:T(512)S(1)}, f32[512]{0:T(512)}, u32[]{:S(2)}) copy-start(f32[512]{0:T(512)} %param.27) | copy-start | bytes 6148
  24.6 10.1 %copy-start.9 = (f32[32,128]{1,0:T(8,128)S(1)}, f32[32,128]{1,0:T(8,128)}, u32[]{:S(2)}) copy-start(f32[32,128]{1,0:T(8,128)} %param.26) | copy-start | bytes 49156
  39.7 9.5 %copy-start.4 = (bf16[1,128,512]{1,2,0:T(8,128)(2,1)S(1)}, bf16[1,128,512]{1,2,0:T(8,128)(2,1)}, u32[]{:S(2)}) copy-start(bf16[1,128,512]{1,2,0:T(8,128)(2,1)} %copy.131) | copy-start | bytes 393220
  39.7 9.6 %copy-start.2 = (bf16[1,128,512]{1,2,0:T(8,128)(2,1)S(1)}, bf16[1,128,512]{1,2,0:T(8,128)(2,1)}, u32[]{:S(2)}) copy-start(bf16[1,128,512]{1,2,0:T(8,128)(2,1)} %copy.137) | copy-start | bytes 393220
  39.7 9.8 %copy-start.6 = (bf16[1,128,512]{1,2,0:T(8,128)(2,1)S(1)}, bf16[1,128,512]{1,2,0:T(8,128)(2,1)}, u32[]{:S(2)}) copy-start(bf16[1,128,512]{1,2,0:T(8,128)(2,1)} %copy.130) | copy-start | bytes 393220
  39.8 9.9 %copy-start.5 = (bf16[1,128,512]{1,2,0:T(8,128)(2,1)S(1)}, bf16[1,128,512]{1,2,0:T(8,128)(2,1)}, u32[]{:S(2)}) copy-start(bf16[1,128,512]{1,2,0:T(8,128)(2,1)} %copy.129) | copy-start | bytes 393220
  94.3 289.2 %collective-permute-start.1 = (bf16[127,512]{1,0:T(8,128)(2,1)S(1)}, bf16[127,512]{1,0:T(8,128)(2,1)S(1)}, u32[]{:S(2)}, u32[]{:S(2)}) collective-permute-start(bf16[127,512]{1,0:T(8,128)(2,1)S(1)} %bitcast.213), channel_id=1, source_target_pairs={{8,0},{16,8},{24,16},{32,24},{40,32},{48,40},{56,48},{64,56},{72,6... | collective-permute-start | bytes 390152 | tf_op jit(solution)/shard_map/ppermute | solution.py:12
  96.6 291.5 %copy-start.7 = (bf16[1,128,512]{2,1,0:T(8,128)(2,1)S(1)}, bf16[1,128,512]{2,1,0:T(8,128)(2,1)}, u32[]{:S(2)}) copy-start(bf16[1,128,512]{2,1,0:T(8,128)(2,1)} %param.24) | copy-start | bytes 393220
  96.6 291.5 %copy-start.8 = (bf16[1,128,512]{2,1,0:T(8,128)(2,1)S(1)}, bf16[1,128,512]{2,1,0:T(8,128)(2,1)}, u32[]{:S(2)}) copy-start(bf16[1,128,512]{2,1,0:T(8,128)(2,1)} %param.22) | copy-start | bytes 393220
  403.6 187.0 %all-to-all-start = ((f32[32,128,4]{1,2,0:T(4,128)}), f32[32,128,4]{1,2,0:T(4,128)S(1)}, u32[]{:S(2)}, u32[]{:S(2)}) async-start(f32[32,128,4]{1,2,0:T(4,128)} %stack.2), calls=%async_computation | async-start | bytes 131072 | tf_op jit(solution)/shard_map/all_to_all | solution.py:201
Sparse Core Ops, SparseCore 0:
  10.6 146.1 all-gather.10
  159.4 137.5 all-gather.8
  299.0 139.1 all-gather.12
  440.6 150.0 all-gather.14
